TPU v7x, 128 devices: a whole 4x4x4 slice. The times are simulated.
128 devices in a mesh: wide: 16 (over x_hi, y, core), narrow: 4 (over z), depth: 2 (over x_lo).
Axes of the slice: x: 4 (x_hi: 2, x_lo: 2; x = x_hi * 2 + x_lo), y: 4, z: 4, core: 2. Of those that a mesh axis runs over, the one named last changes fastest.
Arguments:
- hidden_state: bfloat16 [64, 4096], P(('wide', 'depth')), may hold values from -6 to 6
- query_weight: bfloat16 [4096, 4096], P('depth', 'narrow'), may hold values from -0.09375 to 0.09375
- output_weight: bfloat16 [4096, 4096], P('narrow'), may hold values from -0.09375 to 0.09375
- cache_keys: bfloat16 [64, 512, 4096], P(('wide', 'depth'), None, 'narrow'), may hold values from -128 to 128
- cache_values: bfloat16 [64, 512, 4096], P(('wide', 'depth'), None, 'narrow'), may hold values from -12 to 12
- enc_blocks: int32 [64], replicated, may hold values from 1 to 4
- cache_slot: int32 [64], replicated, may hold values from 0 to 63, as said below
Outputs:
- attended: bfloat16 [64, 4096], P(('wide', 'depth'), 'narrow')
Inputs may be any that keep to these rules, and one draw needn't show every extreme that they name: Request r attends to the first 128 * enc_blocks[r] rows of its cache slot. Every slot holds exactly one request, and r and cache_slot[r] agree in their value of (index // 2) % 2.
All inputs are finite; a program needn't handle non-finite values.
Results may differ from a plain program's by a relative error of at most 0.012.
The roundings to bfloat16 on the way count: a program that leaves them out, or rounds other values in their place, can miss the bound.
Values may be sent and summed in bfloat16 or wider, within the bound.
A program may use at most 64 MiB of HBM per device.

v0:
```python
import jax
import jax.numpy as jnp
from jax import lax
from jax.sharding import PartitionSpec as P

HDIM = 64
BLOCK = 128


def sent_to_all(value, axis):
    copies = jnp.broadcast_to(value, (lax.axis_size(axis), *value.shape))
    return lax.all_to_all(copies, axis, split_axis=0, concat_axis=0, tiled=True)


def joined_along(pieces, dim):
    lengths = list(pieces.shape[1:])
    lengths[dim] *= pieces.shape[0]
    return jnp.moveaxis(pieces, 0, dim).reshape(lengths)


def gathered_copies(value, axis, dim):
    pieces = sent_to_all(value, axis)
    return joined_along(pieces, dim)


def in_blocks(value, dim, size):
    before, after = (value.shape[:dim], value.shape[dim + 1 :])
    return jnp.moveaxis(value.reshape(*before, size, -1, *after), dim, 0)


def sent_and_summed(value, axis, dim):
    pieces = in_blocks(value, dim, lax.axis_size(axis))
    arrived = lax.all_to_all(pieces, axis, split_axis=0, concat_axis=0, tiled=True)
    return arrived.sum(axis=0)


def sum_at_owner(value, axis, dim):
    size = lax.axis_size(axis)
    pieces = lax.all_to_all(in_blocks(value, dim, size), axis, 0, 0, tiled=True)
    return jnp.sum(pieces.astype(jnp.float32), axis=0)


def attend_pairs(queries, key_rows, value_rows, chosen, block_count):
    query_count = queries.shape[0]
    piece_rows, cache_len, features = key_rows.shape
    head_count = features // HDIM
    query_heads = queries.reshape(query_count, head_count, HDIM)
    key_heads = key_rows.reshape(piece_rows, cache_len, head_count, HDIM)
    value_heads = value_rows.reshape(piece_rows, cache_len, head_count, HDIM)
    scores = jnp.einsum(
        "ahd,blhd->abhl", query_heads, key_heads, preferred_element_type=jnp.float32
    )
    usable = jnp.arange(cache_len, dtype=jnp.int32)[None, :] < (block_count * BLOCK)[:, None]
    scores = jnp.where(usable[:, None, None, :], scores, jnp.float32(-1e30))
    row_top = jnp.max(scores, axis=-1, keepdims=True)
    raised = jnp.exp(scores - row_top)
    shares = (raised / jnp.sum(raised, axis=-1, keepdims=True)).astype(jnp.bfloat16)
    shares = shares * chosen[:, :, None, None]
    context = jnp.einsum("abhl,blhd->ahd", shares, value_heads, preferred_element_type=jnp.float32)
    return context.reshape(query_count, features)


def shards(
    hidden_state, query_weight, output_weight, cache_keys, cache_values, enc_blocks, cache_slot
):
    row_count = hidden_state.shape[0]
    halves = lax.axis_size("depth")
    at_depth = lax.axis_index("depth")
    at_wide = lax.axis_index("wide")
    widened = hidden_state.astype(jnp.float32)
    mean_square = jnp.mean(widened * widened, axis=-1, keepdims=True)
    normed = (widened * lax.rsqrt(mean_square + 1e-06)).astype(jnp.bfloat16)
    col_width = query_weight.shape[0]
    columns = lax.dynamic_slice_in_dim(
        gathered_copies(normed, "depth", 0), at_depth * col_width, col_width, 1
    )
    partial_rows = jnp.dot(columns, query_weight, preferred_element_type=jnp.float32)
    query_sum = sent_and_summed(partial_rows, "depth", 0)
    queries = query_sum.astype(jnp.bfloat16)
    piece = gathered_copies(queries, "wide", 0)
    piece_rows = piece.shape[0]
    indices = jnp.arange(piece_rows, dtype=jnp.int32)
    global_rows = (indices // row_count * halves + at_depth) * row_count + indices % row_count
    owner_rows = jnp.take(cache_slot, global_rows)
    block_count = jnp.take(enc_blocks, global_rows)
    is_owner = owner_rows // (halves * row_count) == at_wide
    same_row = (owner_rows % row_count)[:, None] == jnp.arange(row_count, dtype=jnp.int32)[None, :]
    chosen = (is_owner[:, None] & same_row).astype(jnp.bfloat16)
    answered = attend_pairs(piece, cache_keys, cache_values, chosen, block_count)
    context_sum = sum_at_owner(answered.astype(jnp.bfloat16), "wide", 0)
    context = context_sum.astype(jnp.bfloat16)
    partial_value = jnp.dot(context, output_weight, preferred_element_type=jnp.float32)
    return sent_and_summed(partial_value, "narrow", 1).astype(jnp.bfloat16)


def solution(mesh):
    placed = (
        P(("wide", "depth"), None),
        P("depth", "narrow"),
        P("narrow", None),
        P(("wide", "depth"), None, "narrow"),
        P(("wide", "depth"), None, "narrow"),
        P(),
        P(),
    )
    return jax.shard_map(
        shards,
        mesh=mesh,
        in_specs=placed,
        out_specs=P(("wide", "depth"), "narrow"),
        check_vma=False,
    )
```

profile of v0, /device:TPU:1, one launch (start us, length us, event | category | flops | bytes accessed | tf_op | source)
XLA Modules:
  0.0 74.4 jit_solution(16040249950901883469)
XLA Ops:
  0.0 0.0 copy-start
  0.0 0.9 %fusion.24 = f32[2]{0:T(128)S(1)} fusion(bf16[2,4096]{1,0:T(2,128)(2,1)} %param.9), kind=kLoop, calls=%fused_computation.25 | loop fusion | flops 24574 | bytes 16392 | tf_op jit(solution)/shard_map/reduce_sum | solution.py:71
  0.9 0.8 %fusion.25 = bf16[2,4096]{1,0:T(2,128)(2,1)S(1)} fusion(bf16[2,4096]{1,0:T(2,128)(2,1)} %param.9, f32[2]{0:T(128)S(1)} %add_rsqrt_fusion), kind=kLoop, calls=%fused_computation.26 | loop fusion | flops 24576 | bytes 32776 | tf_op jit(solution)/shard_map/convert_element_type | solution.py:72
  1.7 0.6 broadcast_in_dim.23
  2.3 3.3 %all-to-all-start = ((bf16[2,2,4096]{2,1,0:T(2,128)(2,1)}), bf16[2,2,4096]{2,1,0:T(2,128)(2,1)S(1)}, u32[]{:S(2)}, u32[]{:S(2)}) async-start(bf16[2,2,4096]{2,1,0:T(2,128)(2,1)} %broadcast_in_dim.23), calls=%async_computation | async-start | bytes 65536 | tf_op jit(solution)/shard_map/all_to_all | solution.py:12
  5.6 0.0 copy-done
  5.6 0.7 gather_fusion.1
  6.3 1.4 %gather_fusion = s32[32]{0:T(128)S(1)} fusion(s32[64]{0:T(128)} %param.14, s32[1024]{0:T(1024)S(1)} %pad_clamp_fusion), kind=kCustom, calls=%fused_computation.clone | custom fusion | bytes 384 | tf_op jit(solution)/shard_map/jit(_take)/gather | solution.py:85
  7.7 0.1 iota_compare_fusion
  7.8 1.1 %all-to-all-done = bf16[2,2,4096]{2,1,0:T(2,128)(2,1)S(1)} async-done(((bf16[2,2,4096]{2,1,0:T(2,128)(2,1)}), bf16[2,2,4096]{2,1,0:T(2,128)(2,1)S(1)}, u32[]{:S(2)}, u32[]{:S(2)}) %all-to-all-start) | async-done | bytes 32800 | tf_op jit(solution)/shard_map/all_to_all | solution.py:12
  8.9 2.8 %fusion.26 = f32[4,1024]{1,0:T(4,128)S(1)} fusion(bf16[2048,1024]{1,0:T(8,128)(2,1)} %param.10, bf16[4,4096]{1,0:T(4,128)(2,1)S(1)} %reshape.88, s32[]{:T(128)S(6)} %select_n.37), kind=kOutput, calls=%fused_computation.27 | convolution fusion | flops 16777216 | bytes 4227076 | tf_op jit(solution)/shard_map/dot_general | solution.py:77
  11.8 0.6 reshape.89
  12.4 3.2 %all-to-all-start.1 = ((f32[2,2,1024]{2,1,0:T(2,128)}), f32[2,2,1024]{2,1,0:T(2,128)S(1)}, u32[]{:S(2)}, u32[]{:S(2)}) async-start(f32[2,2,1024]{2,1,0:T(2,128)} %reshape.89), calls=%async_computation.1 | async-start | bytes 32768 | tf_op jit(solution)/shard_map/all_to_all | solution.py:33
  15.7 2.7 %all-to-all-done.1 = f32[2,2,1024]{2,1,0:T(2,128)S(1)} async-done(((f32[2,2,1024]{2,1,0:T(2,128)}), f32[2,2,1024]{2,1,0:T(2,128)S(1)}, u32[]{:S(2)}, u32[]{:S(2)}) %all-to-all-start.1) | async-done | bytes 16416 | tf_op jit(solution)/shard_map/all_to_all | solution.py:33
  18.4 0.7 broadcast_in_dim.36
  19.0 10.2 %all-to-all-start.2 = ((bf16[16,2,1024]{2,1,0:T(2,128)(2,1)}), bf16[16,2,1024]{2,1,0:T(2,128)(2,1)S(1)}, u32[]{:S(2)}, u32[]{:S(2)}) async-start(bf16[16,2,1024]{2,1,0:T(2,128)(2,1)} %broadcast_in_dim.36), calls=%async_computation.2 | async-start | bytes 131072 | tf_op jit(solution)/shard_map/all_to_all | solution.py:12
  29.2 2.9 %copy.11 = bf16[2,512,1024]{1,2,0:T(8,128)(2,1)S(1)} copy(bf16[2,512,1024]{2,1,0:T(8,128)(2,1)} %param.12) | data formatting | bytes 4194304 | tf_op args[3]
  32.1 4.0 %copy.14 = bf16[2,512,1024]{1,2,0:T(8,128)(2,1)} copy(bf16[2,512,1024]{2,1,0:T(8,128)(2,1)} %param.13) | data formatting | bytes 4194304 | tf_op args[4]
  36.0 0.5 all-to-all-done.2
  36.5 0.1 reshape_reshape.3
  36.7 0.4 fusion.5
  37.1 0.0 copy-start.1
  37.1 0.7 fusion.36
  37.8 0.9 %copy-done.1 = bf16[2,512,1024]{1,2,0:T(8,128)(2,1)S(1)} copy-done((bf16[2,512,1024]{1,2,0:T(8,128)(2,1)S(1)}, bf16[2,512,1024]{1,2,0:T(8,128)(2,1)}, u32[]{:S(2)}) %copy-start.1) | copy-done | bytes 2097176
  38.7 0.7 fusion.16
  39.4 0.1 copy.16
  39.5 0.8 %convert_element_type.41 = bf16[16,2,1024]{2,1,0:T(2,128)(2,1)} reshape(bf16[32,16,64]{2,1,0:T(8,128)(2,1)S(1)} %copy.16) | data formatting | bytes 131072 | tf_op jit(solution)/shard_map/convert_element_type | solution.py:90
  40.3 6.7 %all-to-all-start.3 = ((bf16[16,2,1024]{2,1,0:T(2,128)(2,1)}), bf16[16,2,1024]{2,1,0:T(2,128)(2,1)S(1)}, u32[]{:S(2)}, u32[]{:S(2)}) async-start(bf16[16,2,1024]{2,1,0:T(2,128)(2,1)} %convert_element_type.41), calls=%async_computation.3 | async-start | bytes 131072 | tf_op jit(solution)/shard_map/all_to_all | solution.py:39
  47.0 12.0 %copy.22 = bf16[4096,1024]{1,0:T(8,128)(2,1)} copy(bf16[4096,1024]{0,1:T(8,128)(2,1)} %bitcast.33) | data formatting | bytes 16777216 | tf_op jit(solution)/shard_map/dot_general | solution.py:92
  59.0 0.0 all-to-all-done.3
  59.0 0.1 reduce_sum.51
  59.1 5.6 %convolution_bitcast_fusion = f32[4,2,1024]{2,1,0:T(2,128)S(1)} fusion(bf16[4,1024,1024]{2,1,0:T(8,128)(2,1)} %bitcast.32, bf16[2,1024]{1,0:T(2,128)(2,1)S(1)} %reduce_sum.51), kind=kOutput, calls=%fused_computation.16 | convolution fusion | flops 16777216 | bytes 8425472 | tf_op jit(solution)/shard_map/dot_general | solution.py:92
  64.7 9.1 %all_to_all.25 = f32[4,2,1024]{2,1,0:T(2,128)S(1)} all-to-all(f32[4,2,1024]{2,1,0:T(2,128)S(1)} %convolution_bitcast_fusion), channel_id=1, replica_groups=mesh['wide'=16,'narrow'=4,'depth'=2] {'narrow'}, dimensions={0} | all-to-all | bytes 65536 | tf_op jit(solution)/shard_map/all_to_all | solution.py:33
  73.8 0.6 reduce_sum.52
  (9 shorter events, 0.1 us)
Async XLA Ops:
  0.0 5.6 %copy-start = (s32[64]{0:T(128)S(1)}, s32[64]{0:T(128)}, u32[]{:S(2)}) copy-start(s32[64]{0:T(128)} %param.15) | copy-start | bytes 772
  2.3 6.6 %all-to-all-start = ((bf16[2,2,4096]{2,1,0:T(2,128)(2,1)}), bf16[2,2,4096]{2,1,0:T(2,128)(2,1)S(1)}, u32[]{:S(2)}, u32[]{:S(2)}) async-start(bf16[2,2,4096]{2,1,0:T(2,128)(2,1)} %broadcast_in_dim.23), calls=%async_computation | async-start | bytes 65536 | tf_op jit(solution)/shard_map/all_to_all | solution.py:12
  12.4 5.9 %all-to-all-start.1 = ((f32[2,2,1024]{2,1,0:T(2,128)}), f32[2,2,1024]{2,1,0:T(2,128)S(1)}, u32[]{:S(2)}, u32[]{:S(2)}) async-start(f32[2,2,1024]{2,1,0:T(2,128)} %reshape.89), calls=%async_computation.1 | async-start | bytes 32768 | tf_op jit(solution)/shard_map/all_to_all | solution.py:33
  19.0 17.5 %all-to-all-start.2 = ((bf16[16,2,1024]{2,1,0:T(2,128)(2,1)}), bf16[16,2,1024]{2,1,0:T(2,128)(2,1)S(1)}, u32[]{:S(2)}, u32[]{:S(2)}) async-start(bf16[16,2,1024]{2,1,0:T(2,128)(2,1)} %broadcast_in_dim.36), calls=%async_computation.2 | async-start | bytes 131072 | tf_op jit(solution)/shard_map/all_to_all | solution.py:12
  37.1 1.6 %copy-start.1 = (bf16[2,512,1024]{1,2,0:T(8,128)(2,1)S(1)}, bf16[2,512,1024]{1,2,0:T(8,128)(2,1)}, u32[]{:S(2)}) copy-start(bf16[2,512,1024]{1,2,0:T(8,128)(2,1)} %copy.14) | copy-start | bytes 6291460
  40.3 18.7 %all-to-all-start.3 = ((bf16[16,2,1024]{2,1,0:T(2,128)(2,1)}), bf16[16,2,1024]{2,1,0:T(2,128)(2,1)S(1)}, u32[]{:S(2)}, u32[]{:S(2)}) async-start(bf16[16,2,1024]{2,1,0:T(2,128)(2,1)} %convert_element_type.41), calls=%async_computation.3 | async-start | bytes 131072 | tf_op jit(solution)/shard_map/all_to_all | solution.py:39
where the time goes:
time: 76 us; the launch traced here: 74.4 us
  local copies, waits for them, and re-layouts  24.6 us (32%)
  starting transfers between devices  23.4 us (31%)
  matrix products  9.65 us (13%)
  blocking collectives  9.14 us (12%)
  waiting for transfers between devices  4.25 us (6%)
  other arithmetic  3.26 us (4%)
    all_to_all x2, starting transfers between devices, sent_to_all(): return lax.all_to_all(copies, axis, split_axis=0, concat_axis=0, tiled=True)  13.5 us
    dot_general x1, local copies, waits for them, and re-layouts, shards(): jnp.dot(context, output_weight, preferred_element_type=jnp.float32)  12 us
    all_to_all x1, blocking collectives, sent_and_summed(): lax.all_to_all(pieces, axis, split_axis=0, concat_axis=0, tiled=True)  9.14 us
    unnamed x6, local copies, waits for them, and re-layouts  7.7 us
    all_to_all x1, starting transfers between devices, sum_at_owner(): pieces = lax.all_to_all(in_blocks(value, dim, size), axis, 0, 0, tiled=True)  6.75 us
    dot_general x1, matrix products, shards(): jnp.dot(context, output_weight, preferred_element_type=jnp.float32)  5.64 us
    all_to_all x1, starting transfers between devices, sent_and_summed(): lax.all_to_all(pieces, axis, split_axis=0, concat_axis=0, tiled=True)  3.23 us
    dot_general x1, matrix products, shards(): jnp.dot(columns, query_weight, preferred_element_type=jnp.float32)  2.85 us
  transfers between devices with their start and end apart: 4, of which 3 were waited for; matrix products, arithmetic and copies ran while one was open for 28% of the time, Pallas kernels for 0%

commit v1 on v0

v1 whole, which is shorter than its diff:
```python
import jax
import jax.numpy as jnp
from jax import lax
from jax.experimental import pallas as pl
from jax.experimental.pallas import tpu as pltpu
from jax.sharding import PartitionSpec as P

HDIM = 64
BLOCK = 128
XH, Y, C = 2, 4, 2
WIDE, NARROW, DEPTH = 16, 4, 2
ROWS = 2
MESH = pl.DeviceIdType.MESH


def kernel(
    hid, wq, wo, keys, vals, enc_blocks, cache_slot, out,
    hid_v, wq_v, wo_v, k_v, v_v,
    norm_own, norm_got, part_out, part_got, q_own, q_all, ctx_v,
    out_part, out_got, fin_all,
    ld_sem, a_send, a_recv, x_send, x_recv, y_send, y_recv, e_send, e_recv, f_send, f_recv,
):
    w = lax.axis_index("wide")
    z = lax.axis_index("narrow")
    d = lax.axis_index("depth")
    xh, y, c = w // 8, (w // 2) % 4, w % 2
    half = wq.shape[0]
    feats = wq.shape[1]
    heads = feats // HDIM

    def wide_of(xh_, y_, c_):
        return xh_ * 8 + y_ * 2 + c_

    def peer(w_, z_, d_):
        return {"wide": w_, "narrow": z_, "depth": d_}

    def remote(src, dst, send, recv, to):
        return pltpu.make_async_remote_copy(
            src_ref=src, dst_ref=dst, send_sem=send, recv_sem=recv, device_id=to, device_id_type=MESH
        )

    ld_hid = pltpu.make_async_copy(hid, hid_v, ld_sem.at[0])
    ld_wq = pltpu.make_async_copy(wq, wq_v, ld_sem.at[1])
    ld_k = pltpu.make_async_copy(keys, k_v, ld_sem.at[2])
    ld_v = pltpu.make_async_copy(vals, v_v, ld_sem.at[3])
    ld_wo = [
        pltpu.make_async_copy(
            wo.at[:, pl.ds(pl.multiple_of((z + dz) % 4 * feats, feats), feats)], wo_v.at[dz], ld_sem.at[4 + dz]
        )
        for dz in range(4)
    ]
    ld_hid.start()
    ld_wq.start()
    ld_k.start()
    ld_v.start()
    for dz in (2, 1, 3, 0):
        ld_wo[dz].start()

    barrier = pltpu.get_barrier_semaphore()
    peers = [peer((w + o) % WIDE, z, d) for o in range(1, WIDE)]
    peers += [peer(w, z, 1 - d), peer(wide_of(1 - xh, y, c), z, 1 - d)]
    peers += [peer(w, (z + o) % NARROW, d) for o in range(1, NARROW)]
    for p in peers:
        pl.semaphore_signal(barrier, inc=1, device_id=p, device_id_type=MESH)

    ld_hid.wait()
    wide_hid = hid_v[...].astype(jnp.float32)
    mean_square = jnp.mean(wide_hid * wide_hid, axis=-1, keepdims=True)
    normed = (wide_hid * lax.rsqrt(mean_square + 1e-06)).astype(jnp.bfloat16)
    norm_own[0] = normed[:, :half]
    norm_own[1] = normed[:, half:]

    slot_req = []
    for i in range(ROWS):
        mine = (w * DEPTH + d) * ROWS + i
        req = jnp.int32(0)
        for j in range(WIDE * ROWS):
            cand = (j // ROWS * DEPTH + d) * ROWS + j % ROWS
            req = jnp.where(cache_slot[cand] == mine, cand, req)
        slot_req.append(req)

    pl.semaphore_wait(barrier, len(peers))

    cp_a = remote(norm_own.at[1 - d], norm_got, a_send, a_recv, peer(w, z, 1 - d))
    cp_a.start()
    ld_wq.wait()
    cp_a.wait_recv()
    lhs = jnp.concatenate(
        [norm_own[d].astype(jnp.float32), norm_got[...].astype(jnp.float32)], axis=0
    ).astype(jnp.bfloat16)
    part = jnp.dot(lhs, wq_v[...], preferred_element_type=jnp.float32)
    part_out[0] = part[:ROWS]
    part_out[1] = part[ROWS:]
    other_w = wide_of(1 - xh, y, c)
    cp_x = [
        remote(part_out.at[0], part_got.at[0], x_send.at[0], x_recv.at[0], peer(other_w, z, d)),
        remote(part_out.at[1], part_got.at[1], x_send.at[1], x_recv.at[1], peer(w, z, 1 - d)),
        remote(part_out.at[1], part_got.at[2], x_send.at[2], x_recv.at[2], peer(other_w, z, 1 - d)),
    ]
    for cp in cp_x:
        cp.start()
    for cp in cp_x:
        cp.wait_recv()
    q_own[xh] = (part_out[0] + part_got[1]).astype(jnp.bfloat16)
    q_own[1 - xh] = (part_got[0] + part_got[2]).astype(jnp.bfloat16)

    yc = y * 2 + c
    cp_y = []
    for o in range(1, Y * C):
        yc_to = (yc + o) % (Y * C)
        cp_y.append(
            remote(q_own, q_all.at[yc], y_send.at[o], y_recv.at[o], peer(xh * 8 + yc_to, z, d))
        )
    for cp in cp_y:
        cp.start()
    q_all[yc] = q_own[...]
    ld_k.wait()
    ld_v.wait()
    for o in range(1, Y * C):
        yc_from = (yc + Y * C - o) % (Y * C)
        remote(q_own, q_all.at[yc_from], y_send.at[o], y_recv.at[o], peer(w, z, d)).wait_recv()

    head_of = lax.broadcasted_iota(jnp.int32, (heads, feats), 1) // HDIM
    own_head = head_of == lax.broadcasted_iota(jnp.int32, (heads, feats), 0)
    row_id = lax.broadcasted_iota(jnp.int32, (ROWS, feats), 0)
    for i in range(ROWS):
        req = slot_req[i]
        src = req // (DEPTH * ROWS)
        pair = q_all[src % 8, src // 8].astype(jnp.float32)
        query = jnp.sum(jnp.where(row_id == req % ROWS, pair, 0.0), axis=0, keepdims=True)
        spread = jnp.where(own_head, query, 0.0).astype(jnp.bfloat16)
        scores = lax.dot_general(
            spread, k_v[i], (((1,), (1,)), ((), ())), preferred_element_type=jnp.float32
        )
        position = lax.broadcasted_iota(jnp.int32, scores.shape, 1)
        scores = jnp.where(position < enc_blocks[req] * BLOCK, scores, -1e30)
        raised = jnp.exp(scores - jnp.max(scores, axis=-1, keepdims=True))
        shares = (raised / jnp.sum(raised, axis=-1, keepdims=True)).astype(jnp.bfloat16)
        ctx = jnp.dot(shares, v_v[i], preferred_element_type=jnp.float32)
        ctx = jnp.sum(jnp.where(own_head, ctx, 0.0), axis=0, keepdims=True)
        ctx_v[pl.ds(i, 1), :] = ctx

    ctx_b = ctx_v[...].astype(jnp.bfloat16)
    cp_e = {}
    for dz in (2, 1, 3):
        ld_wo[dz].wait()
        out_part[dz] = jnp.dot(ctx_b, wo_v[dz], preferred_element_type=jnp.float32)
        cp_e[dz] = remote(
            out_part.at[dz], out_got.at[dz], e_send.at[dz], e_recv.at[dz], peer(w, (z + dz) % NARROW, d)
        )
        cp_e[dz].start()
    ld_wo[0].wait()
    total = jnp.dot(ctx_b, wo_v[0], preferred_element_type=jnp.float32)
    for dz in (1, 3, 2):
        cp_e[dz].wait_recv()
        total = total + out_got[dz]
    fin_all[w] = total.astype(jnp.bfloat16)

    cp_f = []
    for o in range(1, WIDE):
        cp_f.append(
            remote(fin_all.at[w], fin_all.at[w], f_send.at[o], f_recv.at[o], peer((w + o) % WIDE, z, d))
        )
    for cp in cp_f:
        cp.start()
    for o in range(1, WIDE):
        src = (w + WIDE - o) % WIDE
        remote(fin_all.at[src], fin_all.at[src], f_send.at[o], f_recv.at[o], peer(w, z, d)).wait_recv()
    rows = []
    for i in range(ROWS):
        slot = cache_slot[(w * DEPTH + d) * ROWS + i]
        pair = fin_all[slot // (DEPTH * ROWS)].astype(jnp.float32)
        rows.append(jnp.sum(jnp.where(row_id == slot % ROWS, pair, 0.0), axis=0, keepdims=True))
    out[...] = jnp.concatenate(rows, axis=0).astype(jnp.bfloat16)

    cp_a.wait_send()
    for cp in cp_x + cp_y + list(cp_e.values()) + cp_f:
        cp.wait_send()


def shards(hidden_state, query_weight, output_weight, cache_keys, cache_values, enc_blocks, cache_slot):
    rows, width = hidden_state.shape
    half, feats = query_weight.shape
    bf16, f32 = jnp.bfloat16, jnp.float32
    dma = pltpu.SemaphoreType.DMA
    any_spec = pl.BlockSpec(memory_space=pl.ANY)
    smem = pl.BlockSpec(memory_space=pltpu.SMEM)
    return pl.pallas_call(
        kernel,
        out_shape=jax.ShapeDtypeStruct((rows, feats), bf16),
        in_specs=[any_spec] * 5 + [smem] * 2,
        out_specs=pl.BlockSpec(memory_space=pltpu.VMEM),
        scratch_shapes=[
            pltpu.VMEM((rows, width), bf16),
            pltpu.VMEM((half, feats), bf16),
            pltpu.VMEM((NARROW, feats, feats), bf16),
            pltpu.VMEM(cache_keys.shape, bf16),
            pltpu.VMEM(cache_values.shape, bf16),
            pltpu.VMEM((2, rows, half), bf16),
            pltpu.VMEM((rows, half), bf16),
            pltpu.VMEM((2, rows, feats), f32),
            pltpu.VMEM((3, rows, feats), f32),
            pltpu.VMEM((XH, rows, feats), bf16),
            pltpu.VMEM((Y * C, XH, rows, feats), bf16),
            pltpu.VMEM((rows, feats), f32),
            pltpu.VMEM((NARROW, rows, feats), f32),
            pltpu.VMEM((NARROW, rows, feats), f32),
            pltpu.VMEM((WIDE, rows, feats), bf16),
            dma((8,)), dma, dma, dma((3,)), dma((3,)), dma((8,)), dma((8,)),
            dma((4,)), dma((4,)), dma((16,)), dma((16,)),
        ],
        compiler_params=pltpu.CompilerParams(
            collective_id=0, has_side_effects=True, vmem_limit_bytes=48 * 1024 * 1024
        ),
    )(hidden_state, query_weight, output_weight, cache_keys, cache_values, enc_blocks, cache_slot)


def solution(mesh):
    placed = (
        P(("wide", "depth"), None),
        P("depth", "narrow"),
        P("narrow", None),
        P(("wide", "depth"), None, "narrow"),
        P(("wide", "depth"), None, "narrow"),
        P(),
        P(),
    )
    return jax.shard_map(
        shards,
        mesh=mesh,
        in_specs=placed,
        out_specs=P(("wide", "depth"), "narrow"),
        check_vma=False,
    )
```

time: 76 us -> 37.3 us (0.49); the launches traced: 74.4 us -> 37.1 us
  Pallas kernels: 0 us -> 31.2 us
  starting transfers between devices: 23.4 us -> 0 us
  local copies, waits for them, and re-layouts: 24.6 us -> 5.8 us
  matrix products: 9.65 us -> 0 us
  blocking collectives: 9.14 us -> 0 us
  waiting for transfers between devices: 4.25 us -> 0 us
  other arithmetic: 3.26 us -> 0 us
    pallas_call x0 -> x1, Pallas kernels: none -> 31.2 us  [shards(): pl.pallas_call(kernel, out_shape=jax.ShapeDtypeStruct((rows, feats), bf16...]
    all_to_all x4 -> x0, starting transfers between devices: 23.4 us -> none  [the longest x2 13.5 us: sent_to_all(): return lax.all_to_all(copies, axis, split_axis=0, concat_axis=0, tiled=True)]
    dot_general x1 -> x0, local copies, waits for them, and re-layouts: 12 us -> none  [shards(): jnp.dot(context, output_weight, preferred_element_type=jnp.float32)]
    dot_general x4 -> x0, matrix products: 9.65 us -> none  [the longest x1 5.64 us: shards(): jnp.dot(context, output_weight, preferred_element_type=jnp.float32)]
    all_to_all x1 -> x0, blocking collectives: 9.14 us -> none  [sent_and_summed(): lax.all_to_all(pieces, axis, split_axis=0, concat_axis=0, tiled=True)]
    all_to_all x4 -> x0, waiting for transfers between devices: 4.25 us -> none  [the longest x1 2.67 us: sent_and_summed(): lax.all_to_all(pieces, axis, split_axis=0, concat_axis=0, tiled=True)]
    gather x2 -> x0, local copies, waits for them, and re-layouts: 2.06 us -> none  [the longest x1 1.36 us: shards(): block_count = jnp.take(enc_blocks, global_rows)]
    unnamed x6 -> x11, local copies, waits for them, and re-layouts: 7.7 us -> 5.8 us
  transfers between devices with their start and end apart: 4 -> 0, of which waited for: 3 -> 0; matrix products, arithmetic and copies ran while one was open for 28% -> 0% of each run, Pallas kernels for 0% -> 0%
where the time goes in v1:
time: 37.3 us; the launch traced here: 37.1 us
  Pallas kernels  31.2 us (84%)
  local copies, waits for them, and re-layouts  5.8 us (16%)
    pallas_call x1, Pallas kernels, shards(): pl.pallas_call(kernel, out_shape=jax.ShapeDtypeStruct((rows, feats), bf16...  31.2 us
    unnamed x11, local copies, waits for them, and re-layouts  5.8 us

profile of v1, /device:TPU:1, one launch (start us, length us, event | category | flops | bytes accessed | tf_op | source)
XLA Modules:
  0.0 37.1 jit_solution(12843504412072756398)
XLA Ops:
  0.0 0.0 copy-start
  0.0 1.6 %copy-done = bf16[2,512,1024]{2,1,0:T(8,128)(2,1)S(1)} copy-done((bf16[2,512,1024]{2,1,0:T(8,128)(2,1)S(1)}, bf16[2,512,1024]{2,1,0:T(8,128)(2,1)}, u32[]{:S(2)}) %copy-start) | copy-done | bytes 2097176
  1.6 0.0 copy-start.1
  1.6 1.6 %copy-done.1 = bf16[2,512,1024]{2,1,0:T(8,128)(2,1)S(1)} copy-done((bf16[2,512,1024]{2,1,0:T(8,128)(2,1)S(1)}, bf16[2,512,1024]{2,1,0:T(8,128)(2,1)}, u32[]{:S(2)}) %copy-start.1) | copy-done | bytes 2097176
  3.2 0.0 copy-start.2
  3.2 0.7 %copy-done.2 = bf16[2,4096]{1,0:T(2,128)(2,1)S(1)} copy-done((bf16[2,4096]{1,0:T(2,128)(2,1)S(1)}, bf16[2,4096]{1,0:T(2,128)(2,1)}, u32[]{:S(2)}) %copy-start.2) | copy-done | bytes 16408
  3.9 0.0 copy-start.3
  3.9 0.7 %copy-done.3 = s32[64]{0:T(128)S(1)} copy-done((s32[64]{0:T(128)S(1)}, s32[64]{0:T(128)}, u32[]{:S(2)}) %copy-start.3) | copy-done | bytes 280
  4.6 0.0 copy-start.4
  4.6 0.7 %copy-done.4 = s32[64]{0:T(128)S(1)} copy-done((s32[64]{0:T(128)S(1)}, s32[64]{0:T(128)}, u32[]{:S(2)}) %copy-start.4) | copy-done | bytes 280
  5.2 31.2 %shard_map.73 = bf16[2,1024]{1,0:T(2,128)(2,1)S(1)} custom-call(bf16[2,4096]{1,0:T(2,128)(2,1)S(1)} %copy-done.2, bf16[2048,1024]{1,0:T(8,128)(2,1)} %wq.1, bf16[1024,4096]{1,0:T(8,128)(2,1)} %wo.1, bf16[2,512,1024]{2,1,0:T(8,128)(2,1)S(1)} %copy-done, bf16[2,512,1024]{2,1,0:T(8,128)(2,1)S(1)} %copy-done.1, s32[64]{0:T(128)S(1)} %copy-done.3, s32[64]{0:T(128)S(1)} %copy-done.4), custom_call_target="tpu_custom_call" | custom-call | tf_op jit(solution)/shard_map/pallas_call | solution.py:188
  36.5 0.6 %copy.9 = bf16[2,1024]{1,0:T(2,128)(2,1)} copy(bf16[2,1024]{1,0:T(2,128)(2,1)S(1)} %shard_map.73) | data formatting | bytes 8192
Async XLA Ops:
  0.0 1.6 %copy-start = (bf16[2,512,1024]{2,1,0:T(8,128)(2,1)S(1)}, bf16[2,512,1024]{2,1,0:T(8,128)(2,1)}, u32[]{:S(2)}) copy-start(bf16[2,512,1024]{2,1,0:T(8,128)(2,1)} %keys.1) | copy-start | bytes 6291460
  1.6 1.6 %copy-start.1 = (bf16[2,512,1024]{2,1,0:T(8,128)(2,1)S(1)}, bf16[2,512,1024]{2,1,0:T(8,128)(2,1)}, u32[]{:S(2)}) copy-start(bf16[2,512,1024]{2,1,0:T(8,128)(2,1)} %vals.1) | copy-start | bytes 6291460
  3.2 0.7 %copy-start.2 = (bf16[2,4096]{1,0:T(2,128)(2,1)S(1)}, bf16[2,4096]{1,0:T(2,128)(2,1)}, u32[]{:S(2)}) copy-start(bf16[2,4096]{1,0:T(2,128)(2,1)} %hid.1) | copy-start | bytes 49156
  3.9 0.7 %copy-start.3 = (s32[64]{0:T(128)S(1)}, s32[64]{0:T(128)}, u32[]{:S(2)}) copy-start(s32[64]{0:T(128)} %enc_blocks.1) | copy-start | bytes 772
  4.6 0.7 %copy-start.4 = (s32[64]{0:T(128)S(1)}, s32[64]{0:T(128)}, u32[]{:S(2)}) copy-start(s32[64]{0:T(128)} %cache_slot.1) | copy-start | bytes 772

commit v2 on v1

v2 whole, which is shorter than its diff:
```python
import jax
import jax.numpy as jnp
from jax import lax
from jax.experimental import pallas as pl
from jax.experimental.pallas import tpu as pltpu
from jax.sharding import PartitionSpec as P

HDIM = 64
BLOCK = 128
XH, Y, C = 2, 4, 2
WIDE, NARROW, DEPTH = 16, 4, 2
ROWS = 2
MESH = pl.DeviceIdType.MESH
FAR = (2, 1, 3, 0)
STEPS = [(a, b, e) for a in (1, 0) for b in FAR for e in (0, 1)]


def kernel(
    hid, wq, wo, keys, vals, enc_hbm, slot_hbm, out,
    hid_v, wq_v, wo_v, k_v, v_v, enc_blocks, cache_slot,
    norm_own, norm_got, q_own, q_out, q_oth, ctx_v,
    out_part, out_got, fin_all,
    ld_sem, a_send, a_recv, p_send, p_recv, o_send, o_recv, e_send, e_recv, f_send, f_recv,
):
    w = lax.axis_index("wide")
    z = lax.axis_index("narrow")
    d = lax.axis_index("depth")
    xh, y, c = w // 8, (w // 2) % 4, w % 2
    half = wq.shape[0]
    feats = wq.shape[1]
    heads = feats // HDIM

    def wide_at(step, sign):
        return (xh + step[0]) % XH * 8 + (y + sign * step[1] + Y) % Y * 2 + (c + step[2]) % C

    def peer(w_, z_, d_):
        return {"wide": w_, "narrow": z_, "depth": d_}

    def remote(src, dst, send, recv, to):
        return pltpu.make_async_remote_copy(
            src_ref=src, dst_ref=dst, send_sem=send, recv_sem=recv, device_id=to, device_id_type=MESH
        )

    barrier = pltpu.get_barrier_semaphore()
    peers = [peer(wide_at(s, 1), z, d) for s in STEPS if s != (0, 0, 0)]
    peers += [peer(wide_at(s, 1), z, 1 - d) for s in STEPS]
    peers += [peer(w, (z + o) % NARROW, d) for o in range(1, NARROW)]
    for p in peers:
        pl.semaphore_signal(barrier, inc=1, device_id=p, device_id_type=MESH)

    ld_hid = pltpu.make_async_copy(hid, hid_v, ld_sem.at[0])
    ld_wq = pltpu.make_async_copy(wq, wq_v, ld_sem.at[1])
    ld_k = pltpu.make_async_copy(keys, k_v, ld_sem.at[2])
    ld_v = pltpu.make_async_copy(vals, v_v, ld_sem.at[3])
    ld_wo = [
        pltpu.make_async_copy(
            wo.at[:, pl.ds(pl.multiple_of((z + dz) % 4 * feats, feats), feats)], wo_v.at[dz], ld_sem.at[4 + dz]
        )
        for dz in range(4)
    ]
    ld_enc = pltpu.make_async_copy(enc_hbm, enc_blocks, ld_sem.at[8])
    ld_slot = pltpu.make_async_copy(slot_hbm, cache_slot, ld_sem.at[9])
    ld_hid.start()
    ld_enc.start()
    ld_slot.start()
    ld_wq.start()
    ld_k.start()
    ld_v.start()
    for dz in (2, 1, 3, 0):
        ld_wo[dz].start()

    ld_hid.wait()
    wide_hid = hid_v[...].astype(jnp.float32)
    mean_square = jnp.mean(wide_hid * wide_hid, axis=-1, keepdims=True)
    normed = (wide_hid * lax.rsqrt(mean_square + 1e-06)).astype(jnp.bfloat16)
    norm_own[0] = normed[:, :half]
    norm_own[1] = normed[:, half:]

    ld_enc.wait()
    ld_slot.wait()
    slot_req = []
    for i in range(ROWS):
        mine = (w * DEPTH + d) * ROWS + i
        req = jnp.int32(0)
        for j in range(WIDE * ROWS):
            cand = (j // ROWS * DEPTH + d) * ROWS + j % ROWS
            req = jnp.where(cache_slot[cand] == mine, cand, req)
        slot_req.append(req)

    pl.semaphore_wait(barrier, len(peers))
    cp_a = remote(norm_own.at[1 - d], norm_got, a_send, a_recv, peer(w, z, 1 - d))
    cp_a.start()

    ld_wq.wait()
    q_own[w] = jnp.dot(norm_own[d], wq_v[...], preferred_element_type=jnp.float32)
    cp_p = [
        remote(q_own.at[w], q_own.at[w], p_send.at[i], p_recv.at[i], peer(wide_at(s, 1), z, d))
        for i, s in enumerate(STEPS[:-2] + STEPS[-1:])
    ]
    for cp in cp_p:
        cp.start()

    cp_a.wait_recv()
    q_out[...] = jnp.dot(norm_got[...], wq_v[...], preferred_element_type=jnp.float32)
    cp_o = [
        remote(q_out, q_oth.at[w], o_send.at[i], o_recv.at[i], peer(wide_at(s, 1), z, 1 - d))
        for i, s in enumerate(STEPS)
    ]
    for cp in cp_o:
        cp.start()

    ld_k.wait()
    ld_v.wait()
    for i, s in enumerate(STEPS[:-2] + STEPS[-1:]):
        src = wide_at(s, -1)
        remote(q_own.at[src], q_own.at[src], p_send.at[i], p_recv.at[i], peer(w, z, 1 - d)).wait_recv()
    for i, s in enumerate(STEPS):
        src = wide_at(s, -1)
        remote(q_out, q_oth.at[src], o_send.at[i], o_recv.at[i], peer(w, z, 1 - d)).wait_recv()
    head_of = lax.broadcasted_iota(jnp.int32, (heads, feats), 1) // HDIM
    own_head = head_of == lax.broadcasted_iota(jnp.int32, (heads, feats), 0)
    row_id = lax.broadcasted_iota(jnp.int32, (ROWS, feats), 0)
    for i in range(ROWS):
        req = slot_req[i]
        src = req // (DEPTH * ROWS)
        pair = (q_own[src] + q_oth[src]).astype(jnp.bfloat16).astype(jnp.float32)
        query = jnp.sum(jnp.where(row_id == req % ROWS, pair, 0.0), axis=0, keepdims=True)
        spread = jnp.where(own_head, query, 0.0).astype(jnp.bfloat16)
        scores = lax.dot_general(
            spread, k_v[i], (((1,), (1,)), ((), ())), preferred_element_type=jnp.float32
        )
        position = lax.broadcasted_iota(jnp.int32, scores.shape, 1)
        scores = jnp.where(position < enc_blocks[req] * BLOCK, scores, -1e30)
        raised = jnp.exp(scores - jnp.max(scores, axis=-1, keepdims=True))
        shares = (raised / jnp.sum(raised, axis=-1, keepdims=True)).astype(jnp.bfloat16)
        ctx = jnp.dot(shares, v_v[i], preferred_element_type=jnp.float32)
        ctx = jnp.sum(jnp.where(own_head, ctx, 0.0), axis=0, keepdims=True)
        ctx_v[pl.ds(i, 1), :] = ctx
    ctx_b = ctx_v[...].astype(jnp.bfloat16)
    cp_e = {}
    for dz in (2, 1, 3):
        ld_wo[dz].wait()
        out_part[dz] = jnp.dot(ctx_b, wo_v[dz], preferred_element_type=jnp.float32)
        cp_e[dz] = remote(
            out_part.at[dz], out_got.at[dz], e_send.at[dz], e_recv.at[dz], peer(w, (z + dz) % NARROW, d)
        )
        cp_e[dz].start()
    ld_wo[0].wait()
    total = jnp.dot(ctx_b, wo_v[0], preferred_element_type=jnp.float32)
    for dz in (1, 3, 2):
        cp_e[dz].wait_recv()
        total = total + out_got[dz]
    fin_all[w] = total.astype(jnp.bfloat16)
    cp_f = []
    for i, s in enumerate(STEPS[:-2] + STEPS[-1:]):
        cp_f.append(
            remote(fin_all.at[w], fin_all.at[w], f_send.at[i], f_recv.at[i], peer(wide_at(s, 1), z, d))
        )
    for cp in cp_f:
        cp.start()
    for i, s in enumerate(STEPS[:-2] + STEPS[-1:]):
        src = wide_at(s, -1)
        remote(fin_all.at[src], fin_all.at[src], f_send.at[i], f_recv.at[i], peer(w, z, 1 - d)).wait_recv()
    rows = []
    for i in range(ROWS):
        slot = cache_slot[(w * DEPTH + d) * ROWS + i]
        pair = fin_all[slot // (DEPTH * ROWS)].astype(jnp.float32)
        rows.append(jnp.sum(jnp.where(row_id == slot % ROWS, pair, 0.0), axis=0, keepdims=True))
    out[...] = jnp.concatenate(rows, axis=0).astype(jnp.bfloat16)

    for cp in [cp_a] + cp_p + cp_o + list(cp_e.values()) + cp_f:
        cp.wait_send()


def shards(hidden_state, query_weight, output_weight, cache_keys, cache_values, enc_blocks, cache_slot):
    rows, width = hidden_state.shape
    half, feats = query_weight.shape
    bf16, f32 = jnp.bfloat16, jnp.float32
    dma = pltpu.SemaphoreType.DMA
    any_spec = pl.BlockSpec(memory_space=pl.ANY)
    return pl.pallas_call(
        kernel,
        out_shape=jax.ShapeDtypeStruct((rows, feats), bf16),
        in_specs=[any_spec] * 7,
        out_specs=pl.BlockSpec(memory_space=pltpu.VMEM),
        scratch_shapes=[
            pltpu.VMEM((rows, width), bf16),
            pltpu.VMEM((half, feats), bf16),
            pltpu.VMEM((NARROW, feats, feats), bf16),
            pltpu.VMEM(cache_keys.shape, bf16),
            pltpu.VMEM(cache_values.shape, bf16),
            pltpu.SMEM(enc_blocks.shape, jnp.int32),
            pltpu.SMEM(cache_slot.shape, jnp.int32),
            pltpu.VMEM((2, rows, half), bf16),
            pltpu.VMEM((rows, half), bf16),
            pltpu.VMEM((WIDE, rows, feats), f32),
            pltpu.VMEM((rows, feats), f32),
            pltpu.VMEM((WIDE, rows, feats), f32),
            pltpu.VMEM((rows, feats), f32),
            pltpu.VMEM((NARROW, rows, feats), f32),
            pltpu.VMEM((NARROW, rows, feats), f32),
            pltpu.VMEM((WIDE, rows, feats), bf16),
            dma((10,)), dma, dma, dma((15,)), dma((15,)), dma((16,)), dma((16,)),
            dma((4,)), dma((4,)), dma((15,)), dma((15,)),
        ],
        compiler_params=pltpu.CompilerParams(
            collective_id=0, has_side_effects=True, vmem_limit_bytes=67_043_328
        ),
    )(hidden_state, query_weight, output_weight, cache_keys, cache_values, enc_blocks, cache_slot)


def solution(mesh):
    placed = (
        P(("wide", "depth"), None),
        P("depth", "narrow"),
        P("narrow", None),
        P(("wide", "depth"), None, "narrow"),
        P(("wide", "depth"), None, "narrow"),
        P(),
        P(),
    )
    return jax.shard_map(
        shards,
        mesh=mesh,
        in_specs=placed,
        out_specs=P(("wide", "depth"), "narrow"),
        check_vma=False,
    )
```

time: 37.3 us -> 30.4 us (0.82)
  local copies, waits for them, and re-layouts: 5.8 us -> 1.28 us
  Pallas kernels: 31.2 us -> 28.9 us
    unnamed x11 -> x1, local copies, waits for them, and re-layouts: 5.8 us -> 1.28 us
    pallas_call x1, Pallas kernels: 31.2 us -> 28.9 us  [shards(): pl.pallas_call(kernel, out_shape=jax.ShapeDtypeStruct((rows, feats), bf16...]
where the time goes in v2:
time: 30.4 us; the launch traced here: 30.2 us
  Pallas kernels  28.9 us (95%)
  local copies, waits for them, and re-layouts  1.28 us (4%)
    pallas_call x1, Pallas kernels, shards(): pl.pallas_call(kernel, out_shape=jax.ShapeDtypeStruct((rows, feats), bf16...  28.9 us
    unnamed x1, local copies, waits for them, and re-layouts  1.28 us

profile of v2, /device:TPU:1, one launch (start us, length us, event | category | flops | bytes accessed | tf_op | source)
XLA Modules:
  0.0 30.2 jit_solution(7557927224756198987)
XLA Ops:
  0.0 28.9 %shard_map.73 = bf16[2,1024]{1,0:T(2,128)(2,1)} custom-call(bf16[2,4096]{1,0:T(2,128)(2,1)} %hid.1, bf16[2048,1024]{1,0:T(8,128)(2,1)} %wq.1, bf16[1024,4096]{1,0:T(8,128)(2,1)} %wo.1, bf16[2,512,1024]{2,1,0:T(8,128)(2,1)} %keys.1, bf16[2,512,1024]{2,1,0:T(8,128)(2,1)} %vals.1, s32[64]{0:T(128)} %enc_hbm.1, s32[64]{0:T(128)} %slot_hbm.1), custom_call_target="tpu_custom_call" | custom-call | tf_op jit(solution)/shard_map/pallas_call | solution.py:181
  28.9 1.3 %copy.9 = bf16[2,1024]{1,0:T(2,128)(2,1)} copy(bf16[2,1024]{1,0:T(2,128)(2,1)} %shard_map.73) | data formatting | bytes 8192

commit v3 on v2

--- a/solution.py
+++ b/solution.py
@@ -19,8 +19,8 @@
     hid, wq, wo, keys, vals, enc_hbm, slot_hbm, out,
     hid_v, wq_v, wo_v, k_v, v_v, enc_blocks, cache_slot,
     norm_own, norm_got, q_own, q_out, q_oth, ctx_v,
-    out_part, out_got, fin_all,
-    ld_sem, a_send, a_recv, p_send, p_recv, o_send, o_recv, e_send, e_recv, f_send, f_recv,
+    fin_out, fin_all,
+    in_sem, ld_sem, a_send, a_recv, p_send, p_recv, o_send, o_recv, e_send, e_recv,
 ):
     w = lax.axis_index("wide")
     z = lax.axis_index("narrow")
@@ -90,6 +90,8 @@
     pl.semaphore_wait(barrier, len(peers))
     cp_a = remote(norm_own.at[1 - d], norm_got, a_send, a_recv, peer(w, z, 1 - d))
     cp_a.start()
+    for o in range(1, NARROW):
+        pl.semaphore_signal(in_sem, inc=1, device_id=peer(w, (z + o) % NARROW, d), device_id_type=MESH)
 
     ld_wq.wait()
     q_own[w] = jnp.dot(norm_own[d], wq_v[...], preferred_element_type=jnp.float32)
@@ -120,55 +122,60 @@
     head_of = lax.broadcasted_iota(jnp.int32, (heads, feats), 1) // HDIM
     own_head = head_of == lax.broadcasted_iota(jnp.int32, (heads, feats), 0)
     row_id = lax.broadcasted_iota(jnp.int32, (ROWS, feats), 0)
+    scores = []
     for i in range(ROWS):
         req = slot_req[i]
         src = req // (DEPTH * ROWS)
         pair = (q_own[src] + q_oth[src]).astype(jnp.bfloat16).astype(jnp.float32)
         query = jnp.sum(jnp.where(row_id == req % ROWS, pair, 0.0), axis=0, keepdims=True)
         spread = jnp.where(own_head, query, 0.0).astype(jnp.bfloat16)
-        scores = lax.dot_general(
+        score = lax.dot_general(
             spread, k_v[i], (((1,), (1,)), ((), ())), preferred_element_type=jnp.float32
         )
-        position = lax.broadcasted_iota(jnp.int32, scores.shape, 1)
-        scores = jnp.where(position < enc_blocks[req] * BLOCK, scores, -1e30)
-        raised = jnp.exp(scores - jnp.max(scores, axis=-1, keepdims=True))
-        shares = (raised / jnp.sum(raised, axis=-1, keepdims=True)).astype(jnp.bfloat16)
-        ctx = jnp.dot(shares, v_v[i], preferred_element_type=jnp.float32)
-        ctx = jnp.sum(jnp.where(own_head, ctx, 0.0), axis=0, keepdims=True)
-        ctx_v[pl.ds(i, 1), :] = ctx
+        position = lax.broadcasted_iota(jnp.int32, score.shape, 1)
+        scores.append(jnp.where(position < enc_blocks[req] * BLOCK, score, -1e30))
+    scores = jnp.concatenate(scores, axis=0)
+    raised = jnp.exp(scores - jnp.max(scores, axis=-1, keepdims=True))
+    shares = (raised / jnp.sum(raised, axis=-1, keepdims=True)).astype(jnp.bfloat16)
+    for i in range(ROWS):
+        ctx = jnp.dot(shares[i * heads : (i + 1) * heads], v_v[i], preferred_element_type=jnp.float32)
+        ctx_v[pl.ds(i, 1), :] = jnp.sum(jnp.where(own_head, ctx, 0.0), axis=0, keepdims=True)
     ctx_b = ctx_v[...].astype(jnp.bfloat16)
-    cp_e = {}
-    for dz in (2, 1, 3):
+    cp_e = []
+    from_e = []
+    for dz in (2, 1, 3, 0):
         ld_wo[dz].wait()
-        out_part[dz] = jnp.dot(ctx_b, wo_v[dz], preferred_element_type=jnp.float32)
-        cp_e[dz] = remote(
-            out_part.at[dz], out_got.at[dz], e_send.at[dz], e_recv.at[dz], peer(w, (z + dz) % NARROW, d)
-        )
-        cp_e[dz].start()
-    ld_wo[0].wait()
-    total = jnp.dot(ctx_b, wo_v[0], preferred_element_type=jnp.float32)
-    for dz in (1, 3, 2):
-        cp_e[dz].wait_recv()
-        total = total + out_got[dz]
-    fin_all[w] = total.astype(jnp.bfloat16)
-    cp_f = []
-    for i, s in enumerate(STEPS[:-2] + STEPS[-1:]):
-        cp_f.append(
-            remote(fin_all.at[w], fin_all.at[w], f_send.at[i], f_recv.at[i], peer(wide_at(s, 1), z, d))
-        )
-    for cp in cp_f:
-        cp.start()
-    for i, s in enumerate(STEPS[:-2] + STEPS[-1:]):
-        src = wide_at(s, -1)
-        remote(fin_all.at[src], fin_all.at[src], f_send.at[i], f_recv.at[i], peer(w, z, 1 - d)).wait_recv()
+        block = jnp.dot(ctx_b, wo_v[dz], preferred_element_type=jnp.float32).astype(jnp.bfloat16)
+        fin_out[dz] = block
+        if dz == 0:
+            fin_all[0, w] = block
+        if dz == 2:
+            pl.semaphore_wait(in_sem, NARROW - 1)
+        for s in STEPS:
+            if s == (0, 0, 0) and dz == 0:
+                continue
+            i = dz * WIDE + STEPS.index(s)
+            to, src = wide_at(s, 1), wide_at(s, -1)
+            cp_e.append(
+                remote(fin_out.at[dz], fin_all.at[dz, w], e_send.at[i], e_recv.at[i], peer(to, (z + dz) % NARROW, d))
+            )
+            from_e.append(
+                remote(fin_out.at[dz], fin_all.at[dz, src], e_send.at[i], e_recv.at[i], peer(w, z, 1 - d))
+            )
+            cp_e[-1].start()
+    for cp in from_e:
+        cp.wait_recv()
     rows = []
     for i in range(ROWS):
         slot = cache_slot[(w * DEPTH + d) * ROWS + i]
-        pair = fin_all[slot // (DEPTH * ROWS)].astype(jnp.float32)
+        src = slot // (DEPTH * ROWS)
+        pair = fin_all[0, src].astype(jnp.float32)
+        for dz in range(1, NARROW):
+            pair = pair + fin_all[dz, src].astype(jnp.float32)
         rows.append(jnp.sum(jnp.where(row_id == slot % ROWS, pair, 0.0), axis=0, keepdims=True))
     out[...] = jnp.concatenate(rows, axis=0).astype(jnp.bfloat16)
 
-    for cp in [cp_a] + cp_p + cp_o + list(cp_e.values()) + cp_f:
+    for cp in [cp_a] + cp_p + cp_o + cp_e:
         cp.wait_send()
 
 
@@ -177,7 +184,11 @@
     half, feats = query_weight.shape
     bf16, f32 = jnp.bfloat16, jnp.float32
     dma = pltpu.SemaphoreType.DMA
-    any_spec = pl.BlockSpec(memory_space=pl.ANY)
+    any_spec = pl.BlockSpec(memory_space=pltpu.HBM)
+    operands = [
+        pltpu.with_memory_space_constraint(a, pltpu.HBM)
+        for a in (hidden_state, query_weight, output_weight, cache_keys, cache_values, enc_blocks, cache_slot)
+    ]
     return pl.pallas_call(
         kernel,
         out_shape=jax.ShapeDtypeStruct((rows, feats), bf16),
@@ -197,16 +208,16 @@
             pltpu.VMEM((rows, feats), f32),
             pltpu.VMEM((WIDE, rows, feats), f32),
             pltpu.VMEM((rows, feats), f32),
-            pltpu.VMEM((NARROW, rows, feats), f32),
-            pltpu.VMEM((NARROW, rows, feats), f32),
-            pltpu.VMEM((WIDE, rows, feats), bf16),
+            pltpu.VMEM((NARROW, rows, feats), bf16),
+            pltpu.VMEM((NARROW, WIDE, rows, feats), bf16),
+            pltpu.SemaphoreType.REGULAR,
             dma((10,)), dma, dma, dma((15,)), dma((15,)), dma((16,)), dma((16,)),
-            dma((4,)), dma((4,)), dma((15,)), dma((15,)),
+            dma((64,)), dma((64,)),
         ],
         compiler_params=pltpu.CompilerParams(
-            collective_id=0, has_side_effects=True, vmem_limit_bytes=67_043_328
+            collective_id=0, has_side_effects=True, vmem_limit_bytes=48 * 1024 * 1024
         ),
-    )(hidden_state, query_weight, output_weight, cache_keys, cache_values, enc_blocks, cache_slot)
+    )(*operands)
 
 
 def solution(mesh):

time: 30.4 us -> 27.5 us (0.905)
  Pallas kernels: 28.9 us -> 26.7 us
  local copies, waits for them, and re-layouts: 1.28 us -> 0.6 us
    pallas_call x1, Pallas kernels: 28.9 us -> 26.7 us  [shards(): pl.pallas_call(kernel, out_shape=jax.ShapeDtypeStruct((rows, feats), bf16...]
    unnamed x1, local copies, waits for them, and re-layouts: 1.28 us -> 0.6 us
where the time goes in v3:
time: 27.5 us; the launch traced here: 27.3 us
  Pallas kernels  26.7 us (97%)
  local copies, waits for them, and re-layouts  0.6 us (2%)
    pallas_call x1, Pallas kernels, shards(): pl.pallas_call(kernel, out_shape=jax.ShapeDtypeStruct((rows, feats), bf16...  26.7 us
    unnamed x1, local copies, waits for them, and re-layouts  0.6 us

profile of v3, /device:TPU:1, one launch (start us, length us, event | category | flops | bytes accessed | tf_op | source)
XLA Modules:
  0.0 27.3 jit_solution(13918935854107352632)
XLA Ops:
  0.0 26.7 %shard_map.73 = bf16[2,1024]{1,0:T(2,128)(2,1)S(1)} custom-call(bf16[2,4096]{1,0:T(2,128)(2,1)} %hid.1, bf16[2048,1024]{1,0:T(8,128)(2,1)} %wq.1, bf16[1024,4096]{1,0:T(8,128)(2,1)} %wo.1, bf16[2,512,1024]{2,1,0:T(8,128)(2,1)} %keys.1, bf16[2,512,1024]{2,1,0:T(8,128)(2,1)} %vals.1, s32[64]{0:T(128)} %enc_hbm.1, s32[64]{0:T(128)} %slot_hbm.1), custom_call_target="tpu_custom_call" | custom-call | tf_op jit(solution)/shard_map/pallas_call | solution.py:192
  26.8 0.6 %copy.9 = bf16[2,1024]{1,0:T(2,128)(2,1)} copy(bf16[2,1024]{1,0:T(2,128)(2,1)S(1)} %shard_map.73) | data formatting | bytes 8192

commit v4 on v3

v4 whole, which is shorter than its diff:
```python
import jax
import jax.numpy as jnp
from jax import lax
from jax.experimental import pallas as pl
from jax.experimental.pallas import tpu as pltpu
from jax.sharding import PartitionSpec as P

HDIM = 64
BLOCK = 128
XH, Y, C = 2, 4, 2
WIDE, NARROW, DEPTH = 16, 4, 2
ROWS = 2
MESH = pl.DeviceIdType.MESH
STEPS = [(a, b, e) for a in (1, 0) for b in (2, 1, 3, 0) for e in (1, 0)]
HOPS = STEPS[:-1]


def kernel(
    hid, wq, wo, keys, vals, enc_hbm, slot_hbm, out,
    hid_v, wq_v, wo_v, k_v, v_v, enc_blocks, cache_slot,
    norm_own, norm_got, q_own, q_out, q_oth, ctx_v, fin_out, fin_all,
    in_sem, ld_sem, send_sem, recv_sem,
):
    w = lax.axis_index("wide")
    z = lax.axis_index("narrow")
    d = lax.axis_index("depth")
    xh, y, c = w // 8, (w // 2) % 4, w % 2
    half = wq.shape[0]
    feats = wq.shape[1]
    cols = feats // C
    heads = feats // HDIM

    def wide_at(step):
        return (xh + step[0]) % XH * 8 + (y + step[1]) % Y * 2 + (c + step[2]) % C

    def peer(w_, z_, d_):
        return {"wide": w_, "narrow": z_, "depth": d_}

    def send(src, dst, which, to):
        cp = pltpu.make_async_remote_copy(
            src_ref=src, dst_ref=dst, send_sem=send_sem.at[which], recv_sem=recv_sem.at[which],
            device_id=to, device_id_type=MESH,
        )
        cp.start()

    def wait_bytes(ref, sem):
        pltpu.make_async_copy(ref, ref, sem).wait()

    barrier = pltpu.get_barrier_semaphore()
    peers = [peer(wide_at(s), z, d) for s in HOPS]
    peers += [peer(wide_at(s), z, 1 - d) for s in STEPS]
    peers += [peer(w, (z + o) % NARROW, d) for o in (2, 1, 3)]
    for p in peers:
        pl.semaphore_signal(barrier, inc=1, device_id=p, device_id_type=MESH)

    ld_hid = pltpu.make_async_copy(hid, hid_v, ld_sem.at[0])
    ld_wq = pltpu.make_async_copy(wq, wq_v, ld_sem.at[1])
    ld_k = pltpu.make_async_copy(keys, k_v, ld_sem.at[2])
    ld_v = pltpu.make_async_copy(vals, v_v, ld_sem.at[3])
    ld_wo = [
        pltpu.make_async_copy(
            wo.at[:, pl.ds(pl.multiple_of((z + dz) % 4 * feats, feats), feats)], wo_v.at[dz], ld_sem.at[4 + dz]
        )
        for dz in range(4)
    ]
    ld_enc = pltpu.make_async_copy(enc_hbm, enc_blocks, ld_sem.at[8])
    ld_slot = pltpu.make_async_copy(slot_hbm, cache_slot, ld_sem.at[9])
    for cp in [ld_hid, ld_enc, ld_slot, ld_wq, ld_k, ld_v, ld_wo[2], ld_wo[1], ld_wo[3], ld_wo[0]]:
        cp.start()

    ld_hid.wait()
    wide_hid = hid_v[...].astype(jnp.float32)
    mean_square = jnp.mean(wide_hid * wide_hid, axis=-1, keepdims=True)
    normed = (wide_hid * lax.rsqrt(mean_square + 1e-06)).astype(jnp.bfloat16)
    norm_own[0] = normed[:, :half]
    norm_own[1] = normed[:, half:]

    ld_enc.wait()
    ld_slot.wait()
    slot_req = []
    for i in range(ROWS):
        mine = (w * DEPTH + d) * ROWS + i
        req = jnp.int32(0)
        for j in range(WIDE * ROWS):
            cand = (j // ROWS * DEPTH + d) * ROWS + j % ROWS
            req = jnp.where(cache_slot[cand] == mine, cand, req)
        slot_req.append(req)

    def sent_a():
        wait_bytes(norm_got, send_sem.at[0])

    def sent_q():
        wait_bytes(q_own.at[pl.ds(0, WIDE - 1)], send_sem.at[1])

    def sent_o():
        wait_bytes(q_oth, send_sem.at[2])

    pl.semaphore_wait(barrier, len(peers))
    for e in range(C):
        send(norm_own.at[1 - d], norm_got.at[c], 0, peer(wide_at((0, 0, e)), z, 1 - d))
    for o in range(1, NARROW):
        pl.semaphore_signal(in_sem, inc=1, device_id=peer(w, (z + o) % NARROW, d), device_id_type=MESH)

    ld_wq.wait()
    q_own[w] = jnp.dot(norm_own[d], wq_v[...], preferred_element_type=jnp.float32)
    for s in HOPS:
        send(q_own.at[w], q_own.at[w], 1, peer(wide_at(s), z, d))

    wait_bytes(norm_got, recv_sem.at[0])
    both = jnp.concatenate([norm_got[e].astype(jnp.float32) for e in range(C)], axis=0).astype(jnp.bfloat16)
    part = jnp.dot(
        both, wq_v[:, pl.ds(pl.multiple_of(c * cols, cols), cols)], preferred_element_type=jnp.float32
    )
    for e in range(C):
        q_out[e] = part[e * ROWS : (e + 1) * ROWS]
    for s in STEPS:
        send(q_out, q_oth.at[c, pl.ds(w // C * C, C)], 2, peer(wide_at(s), z, 1 - d))

    ld_k.wait()
    ld_v.wait()
    wait_bytes(q_own.at[pl.ds(0, WIDE - 1)], recv_sem.at[1])
    wait_bytes(q_oth, recv_sem.at[2])
    head_of = lax.broadcasted_iota(jnp.int32, (heads, feats), 1) // HDIM
    own_head = head_of == lax.broadcasted_iota(jnp.int32, (heads, feats), 0)
    row_id = lax.broadcasted_iota(jnp.int32, (ROWS, feats), 0)
    scores = []
    for i in range(ROWS):
        req = slot_req[i]
        src = req // (DEPTH * ROWS)
        other = jnp.concatenate([q_oth[e, src] for e in range(C)], axis=1)
        pair = (q_own[src] + other).astype(jnp.bfloat16).astype(jnp.float32)
        query = jnp.sum(jnp.where(row_id == req % ROWS, pair, 0.0), axis=0, keepdims=True)
        spread = jnp.where(own_head, query, 0.0).astype(jnp.bfloat16)
        score = lax.dot_general(
            spread, k_v[i], (((1,), (1,)), ((), ())), preferred_element_type=jnp.float32
        )
        position = lax.broadcasted_iota(jnp.int32, score.shape, 1)
        scores.append(jnp.where(position < enc_blocks[req] * BLOCK, score, -1e30))
    scores = jnp.concatenate(scores, axis=0)
    raised = jnp.exp(scores - jnp.max(scores, axis=-1, keepdims=True))
    shares = (raised / jnp.sum(raised, axis=-1, keepdims=True)).astype(jnp.bfloat16)
    for i in range(ROWS):
        ctx = jnp.dot(shares[i * heads : (i + 1) * heads], v_v[i], preferred_element_type=jnp.float32)
        ctx_v[pl.ds(i, 1), :] = jnp.sum(jnp.where(own_head, ctx, 0.0), axis=0, keepdims=True)
    ctx_b = ctx_v[...].astype(jnp.bfloat16)
    for dz in (2, 1, 3, 0):
        ld_wo[dz].wait()
        block = jnp.dot(ctx_b, wo_v[dz], preferred_element_type=jnp.float32).astype(jnp.bfloat16)
        fin_out[dz] = block
        if dz == 0:
            fin_all[w] = block
        if dz == 2:
            pl.semaphore_wait(in_sem, NARROW - 1)
        for s in HOPS if dz == 0 else STEPS:
            send(fin_out.at[dz], fin_all.at[dz * WIDE + w], 3, peer(wide_at(s), (z + dz) % NARROW, d))
    wait_bytes(fin_all.at[pl.ds(0, NARROW * WIDE - 1)], recv_sem.at[3])
    rows = []
    for i in range(ROWS):
        slot = cache_slot[(w * DEPTH + d) * ROWS + i]
        src = slot // (DEPTH * ROWS)
        pair = fin_all[src].astype(jnp.float32)
        for dz in range(1, NARROW):
            pair = pair + fin_all[dz * WIDE + src].astype(jnp.float32)
        rows.append(jnp.sum(jnp.where(row_id == slot % ROWS, pair, 0.0), axis=0, keepdims=True))
    out[...] = jnp.concatenate(rows, axis=0).astype(jnp.bfloat16)

    sent_a()
    sent_q()
    sent_o()
    wait_bytes(fin_all.at[pl.ds(0, NARROW * WIDE - 1)], send_sem.at[3])


def shards(hidden_state, query_weight, output_weight, cache_keys, cache_values, enc_blocks, cache_slot):
    rows, width = hidden_state.shape
    half, feats = query_weight.shape
    bf16, f32 = jnp.bfloat16, jnp.float32
    dma = pltpu.SemaphoreType.DMA
    operands = [
        pltpu.with_memory_space_constraint(a, pltpu.HBM)
        for a in (hidden_state, query_weight, output_weight, cache_keys, cache_values, enc_blocks, cache_slot)
    ]
    return pl.pallas_call(
        kernel,
        out_shape=jax.ShapeDtypeStruct((rows, feats), bf16),
        in_specs=[pl.BlockSpec(memory_space=pltpu.HBM)] * 7,
        out_specs=pl.BlockSpec(memory_space=pltpu.VMEM),
        scratch_shapes=[
            pltpu.VMEM((rows, width), bf16),
            pltpu.VMEM((half, feats), bf16),
            pltpu.VMEM((NARROW, feats, feats), bf16),
            pltpu.VMEM(cache_keys.shape, bf16),
            pltpu.VMEM(cache_values.shape, bf16),
            pltpu.SMEM(enc_blocks.shape, jnp.int32),
            pltpu.SMEM(cache_slot.shape, jnp.int32),
            pltpu.VMEM((2, rows, half), bf16),
            pltpu.VMEM((C, rows, half), bf16),
            pltpu.VMEM((WIDE, rows, feats), f32),
            pltpu.VMEM((C, rows, feats // C), f32),
            pltpu.VMEM((C, WIDE, rows, feats // C), f32),
            pltpu.VMEM((rows, feats), f32),
            pltpu.VMEM((NARROW, rows, feats), bf16),
            pltpu.VMEM((NARROW * WIDE, rows, feats), bf16),
            pltpu.SemaphoreType.REGULAR,
            dma((10,)), dma((4,)), dma((4,)),
        ],
        compiler_params=pltpu.CompilerParams(
            collective_id=0, has_side_effects=True, vmem_limit_bytes=48 * 1024 * 1024
        ),
    )(*operands)


def solution(mesh):
    placed = (
        P(("wide", "depth"), None),
        P("depth", "narrow"),
        P("narrow", None),
        P(("wide", "depth"), None, "narrow"),
        P(("wide", "depth"), None, "narrow"),
        P(),
        P(),
    )
    return jax.shard_map(
        shards,
        mesh=mesh,
        in_specs=placed,
        out_specs=P(("wide", "depth"), "narrow"),
        check_vma=False,
    )
```

time: 27.5 us -> 25.5 us (0.927)
  Pallas kernels: 26.7 us -> 24.7 us
    pallas_call x1, Pallas kernels: 26.7 us -> 24.7 us  [shards(): pl.pallas_call(kernel, out_shape=jax.ShapeDtypeStruct((rows, feats), bf16...]
where the time goes in v4:
time: 25.5 us; the launch traced here: 25.3 us
  Pallas kernels  24.7 us (97%)
  local copies, waits for them, and re-layouts  0.6 us (2%)
    pallas_call x1, Pallas kernels, shards(): pl.pallas_call(kernel, out_shape=jax.ShapeDtypeStruct((rows, feats), bf16...  24.7 us
    unnamed x1, local copies, waits for them, and re-layouts  0.6 us

profile of v4, /device:TPU:1, one launch (start us, length us, event | category | flops | bytes accessed | tf_op | source)
XLA Modules:
  0.0 25.3 jit_solution(11530298422006070701)
XLA Ops:
  0.0 24.7 %shard_map.73 = bf16[2,1024]{1,0:T(2,128)(2,1)S(1)} custom-call(bf16[2,4096]{1,0:T(2,128)(2,1)} %hid.1, bf16[2048,1024]{1,0:T(8,128)(2,1)} %wq.1, bf16[1024,4096]{1,0:T(8,128)(2,1)} %wo.1, bf16[2,512,1024]{2,1,0:T(8,128)(2,1)} %keys.1, bf16[2,512,1024]{2,1,0:T(8,128)(2,1)} %vals.1, s32[64]{0:T(128)} %enc_hbm.1, s32[64]{0:T(128)} %slot_hbm.1), custom_call_target="tpu_custom_call" | custom-call | tf_op jit(solution)/shard_map/pallas_call | solution.py:182
  24.7 0.6 %copy.9 = bf16[2,1024]{1,0:T(2,128)(2,1)} copy(bf16[2,1024]{1,0:T(2,128)(2,1)S(1)} %shard_map.73) | data formatting | bytes 8192

commit v5 on v4

--- a/solution.py
+++ b/solution.py
@@ -27,7 +27,6 @@
     xh, y, c = w // 8, (w // 2) % 4, w % 2
     half = wq.shape[0]
     feats = wq.shape[1]
-    cols = feats // C
     heads = feats // HDIM
 
     def wide_at(step):
@@ -59,13 +58,13 @@
     ld_v = pltpu.make_async_copy(vals, v_v, ld_sem.at[3])
     ld_wo = [
         pltpu.make_async_copy(
-            wo.at[:, pl.ds(pl.multiple_of((z + dz) % 4 * feats, feats), feats)], wo_v.at[dz], ld_sem.at[4 + dz]
+            wo.at[:, pl.ds(dz * feats, feats)], wo_v.at[dz], ld_sem.at[4 + dz]
         )
         for dz in range(4)
     ]
     ld_enc = pltpu.make_async_copy(enc_hbm, enc_blocks, ld_sem.at[8])
     ld_slot = pltpu.make_async_copy(slot_hbm, cache_slot, ld_sem.at[9])
-    for cp in [ld_hid, ld_enc, ld_slot, ld_wq, ld_k, ld_v, ld_wo[2], ld_wo[1], ld_wo[3], ld_wo[0]]:
+    for cp in [ld_hid, ld_enc, ld_slot, ld_wq, ld_k, ld_v, *ld_wo]:
         cp.start()
 
     ld_hid.wait()
@@ -96,8 +95,7 @@
         wait_bytes(q_oth, send_sem.at[2])
 
     pl.semaphore_wait(barrier, len(peers))
-    for e in range(C):
-        send(norm_own.at[1 - d], norm_got.at[c], 0, peer(wide_at((0, 0, e)), z, 1 - d))
+    send(norm_own.at[1 - d], norm_got, 0, peer(w, z, 1 - d))
     for o in range(1, NARROW):
         pl.semaphore_signal(in_sem, inc=1, device_id=peer(w, (z + o) % NARROW, d), device_id_type=MESH)
 
@@ -107,14 +105,9 @@
         send(q_own.at[w], q_own.at[w], 1, peer(wide_at(s), z, d))
 
     wait_bytes(norm_got, recv_sem.at[0])
-    both = jnp.concatenate([norm_got[e].astype(jnp.float32) for e in range(C)], axis=0).astype(jnp.bfloat16)
-    part = jnp.dot(
-        both, wq_v[:, pl.ds(pl.multiple_of(c * cols, cols), cols)], preferred_element_type=jnp.float32
-    )
-    for e in range(C):
-        q_out[e] = part[e * ROWS : (e + 1) * ROWS]
+    q_out[...] = jnp.dot(norm_got[...], wq_v[...], preferred_element_type=jnp.float32)
     for s in STEPS:
-        send(q_out, q_oth.at[c, pl.ds(w // C * C, C)], 2, peer(wide_at(s), z, 1 - d))
+        send(q_out, q_oth.at[w], 2, peer(wide_at(s), z, 1 - d))
 
     ld_k.wait()
     ld_v.wait()
@@ -127,8 +120,7 @@
     for i in range(ROWS):
         req = slot_req[i]
         src = req // (DEPTH * ROWS)
-        other = jnp.concatenate([q_oth[e, src] for e in range(C)], axis=1)
-        pair = (q_own[src] + other).astype(jnp.bfloat16).astype(jnp.float32)
+        pair = (q_own[src] + q_oth[src]).astype(jnp.bfloat16).astype(jnp.float32)
         query = jnp.sum(jnp.where(row_id == req % ROWS, pair, 0.0), axis=0, keepdims=True)
         spread = jnp.where(own_head, query, 0.0).astype(jnp.bfloat16)
         score = lax.dot_general(
@@ -143,24 +135,29 @@
         ctx = jnp.dot(shares[i * heads : (i + 1) * heads], v_v[i], preferred_element_type=jnp.float32)
         ctx_v[pl.ds(i, 1), :] = jnp.sum(jnp.where(own_head, ctx, 0.0), axis=0, keepdims=True)
     ctx_b = ctx_v[...].astype(jnp.bfloat16)
-    for dz in (2, 1, 3, 0):
-        ld_wo[dz].wait()
-        block = jnp.dot(ctx_b, wo_v[dz], preferred_element_type=jnp.float32).astype(jnp.bfloat16)
-        fin_out[dz] = block
-        if dz == 0:
-            fin_all[w] = block
-        if dz == 2:
+    here = z * WIDE + w
+    for to_z in range(NARROW):
+        ld_wo[to_z].wait()
+        block = jnp.dot(ctx_b, wo_v[to_z], preferred_element_type=jnp.float32).astype(jnp.bfloat16)
+        fin_out[to_z] = block
+        if to_z == 0:
             pl.semaphore_wait(in_sem, NARROW - 1)
-        for s in HOPS if dz == 0 else STEPS:
-            send(fin_out.at[dz], fin_all.at[dz * WIDE + w], 3, peer(wide_at(s), (z + dz) % NARROW, d))
+        for s in HOPS:
+            send(fin_out.at[to_z], fin_all.at[here], 3, peer(wide_at(s), to_z, d))
+
+        @pl.when(z != to_z)
+        def _():
+            send(fin_out.at[to_z], fin_all.at[here], 3, peer(w, to_z, d))
+
+    fin_all[here] = fin_out[z]
     wait_bytes(fin_all.at[pl.ds(0, NARROW * WIDE - 1)], recv_sem.at[3])
     rows = []
     for i in range(ROWS):
         slot = cache_slot[(w * DEPTH + d) * ROWS + i]
         src = slot // (DEPTH * ROWS)
         pair = fin_all[src].astype(jnp.float32)
-        for dz in range(1, NARROW):
-            pair = pair + fin_all[dz * WIDE + src].astype(jnp.float32)
+        for from_z in range(1, NARROW):
+            pair = pair + fin_all[from_z * WIDE + src].astype(jnp.float32)
         rows.append(jnp.sum(jnp.where(row_id == slot % ROWS, pair, 0.0), axis=0, keepdims=True))
     out[...] = jnp.concatenate(rows, axis=0).astype(jnp.bfloat16)
 
@@ -193,10 +190,10 @@
             pltpu.SMEM(enc_blocks.shape, jnp.int32),
             pltpu.SMEM(cache_slot.shape, jnp.int32),
             pltpu.VMEM((2, rows, half), bf16),
-            pltpu.VMEM((C, rows, half), bf16),
+            pltpu.VMEM((rows, half), bf16),
             pltpu.VMEM((WIDE, rows, feats), f32),
-            pltpu.VMEM((C, rows, feats // C), f32),
-            pltpu.VMEM((C, WIDE, rows, feats // C), f32),
+            pltpu.VMEM((rows, feats), f32),
+            pltpu.VMEM((WIDE, rows, feats), f32),
             pltpu.VMEM((rows, feats), f32),
             pltpu.VMEM((NARROW, rows, feats), bf16),
             pltpu.VMEM((NARROW * WIDE, rows, feats), bf16),

time: 25.5 us -> 24.9 us (0.976)
  Pallas kernels: 24.7 us -> 24.1 us
    pallas_call x1, Pallas kernels: 24.7 us -> 24.1 us  [shards(): pl.pallas_call(kernel, out_shape=jax.ShapeDtypeStruct((rows, feats), bf16...]
where the time goes in v5:
time: 24.9 us; the launch traced here: 24.7 us
  Pallas kernels  24.1 us (97%)
  local copies, waits for them, and re-layouts  0.6 us (2%)
    pallas_call x1, Pallas kernels, shards(): pl.pallas_call(kernel, out_shape=jax.ShapeDtypeStruct((rows, feats), bf16...  24.1 us
    unnamed x1, local copies, waits for them, and re-layouts  0.6 us

profile of v5, /device:TPU:1, one launch (start us, length us, event | category | flops | bytes accessed | tf_op | source)
XLA Modules:
  0.0 24.7 jit_solution(10358047516083559637)
XLA Ops:
  0.0 24.1 %shard_map.73 = bf16[2,1024]{1,0:T(2,128)(2,1)S(1)} custom-call(bf16[2,4096]{1,0:T(2,128)(2,1)} %hid.1, bf16[2048,1024]{1,0:T(8,128)(2,1)} %wq.1, bf16[1024,4096]{1,0:T(8,128)(2,1)} %wo.1, bf16[2,512,1024]{2,1,0:T(8,128)(2,1)} %keys.1, bf16[2,512,1024]{2,1,0:T(8,128)(2,1)} %vals.1, s32[64]{0:T(128)} %enc_hbm.1, s32[64]{0:T(128)} %slot_hbm.1), custom_call_target="tpu_custom_call" | custom-call | tf_op jit(solution)/shard_map/pallas_call | solution.py:179
  24.1 0.6 %copy.9 = bf16[2,1024]{1,0:T(2,128)(2,1)} copy(bf16[2,1024]{1,0:T(2,128)(2,1)S(1)} %shard_map.73) | data formatting | bytes 8192

commit v6 on v5

--- a/solution.py
+++ b/solution.py
@@ -45,13 +45,6 @@
     def wait_bytes(ref, sem):
         pltpu.make_async_copy(ref, ref, sem).wait()
 
-    barrier = pltpu.get_barrier_semaphore()
-    peers = [peer(wide_at(s), z, d) for s in HOPS]
-    peers += [peer(wide_at(s), z, 1 - d) for s in STEPS]
-    peers += [peer(w, (z + o) % NARROW, d) for o in (2, 1, 3)]
-    for p in peers:
-        pl.semaphore_signal(barrier, inc=1, device_id=p, device_id_type=MESH)
-
     ld_hid = pltpu.make_async_copy(hid, hid_v, ld_sem.at[0])
     ld_wq = pltpu.make_async_copy(wq, wq_v, ld_sem.at[1])
     ld_k = pltpu.make_async_copy(keys, k_v, ld_sem.at[2])
@@ -64,8 +57,15 @@
     ]
     ld_enc = pltpu.make_async_copy(enc_hbm, enc_blocks, ld_sem.at[8])
     ld_slot = pltpu.make_async_copy(slot_hbm, cache_slot, ld_sem.at[9])
-    for cp in [ld_hid, ld_enc, ld_slot, ld_wq, ld_k, ld_v, *ld_wo]:
+    for cp in [ld_hid, ld_enc, ld_slot, ld_wq]:
         cp.start()
+
+    barrier = pltpu.get_barrier_semaphore()
+    peers = [peer(wide_at(s), z, d) for s in HOPS]
+    peers += [peer(wide_at(s), z, 1 - d) for s in STEPS]
+    peers += [peer(w, (z + o) % NARROW, d) for o in (2, 1, 3)]
+    for p in peers:
+        pl.semaphore_signal(barrier, inc=1, device_id=p, device_id_type=MESH)
 
     ld_hid.wait()
     wide_hid = hid_v[...].astype(jnp.float32)
@@ -100,6 +100,8 @@
         pl.semaphore_signal(in_sem, inc=1, device_id=peer(w, (z + o) % NARROW, d), device_id_type=MESH)
 
     ld_wq.wait()
+    for cp in [ld_k, ld_v, *ld_wo]:
+        cp.start()
     q_own[w] = jnp.dot(norm_own[d], wq_v[...], preferred_element_type=jnp.float32)
     for s in HOPS:
         send(q_own.at[w], q_own.at[w], 1, peer(wide_at(s), z, d))

time: 24.9 us -> 24.9 us (level)
  no operation moved by 1% of the time
where the time goes in v6:
time: 24.9 us; the launch traced here: 24.7 us
  Pallas kernels  24.1 us (97%)
  local copies, waits for them, and re-layouts  0.6 us (2%)
    pallas_call x1, Pallas kernels, shards(): pl.pallas_call(kernel, out_shape=jax.ShapeDtypeStruct((rows, feats), bf16...  24.1 us
    unnamed x1, local copies, waits for them, and re-layouts  0.6 us

profile of v6, /device:TPU:1, one launch (start us, length us, event | category | flops | bytes accessed | tf_op | source)
XLA Modules:
  0.0 24.7 jit_solution(9347279500464434279)
XLA Ops:
  0.0 24.1 %shard_map.73 = bf16[2,1024]{1,0:T(2,128)(2,1)S(1)} custom-call(bf16[2,4096]{1,0:T(2,128)(2,1)} %hid.1, bf16[2048,1024]{1,0:T(8,128)(2,1)} %wq.1, bf16[1024,4096]{1,0:T(8,128)(2,1)} %wo.1, bf16[2,512,1024]{2,1,0:T(8,128)(2,1)} %keys.1, bf16[2,512,1024]{2,1,0:T(8,128)(2,1)} %vals.1, s32[64]{0:T(128)} %enc_hbm.1, s32[64]{0:T(128)} %slot_hbm.1), custom_call_target="tpu_custom_call" | custom-call | tf_op jit(solution)/shard_map/pallas_call | solution.py:181
  24.1 0.6 %copy.9 = bf16[2,1024]{1,0:T(2,128)(2,1)} copy(bf16[2,1024]{1,0:T(2,128)(2,1)S(1)} %shard_map.73) | data formatting | bytes 8192

commit v7 on v6

--- a/solution.py
+++ b/solution.py
@@ -17,7 +17,7 @@
 
 def kernel(
     hid, wq, wo, keys, vals, enc_hbm, slot_hbm, out,
-    hid_v, wq_v, wo_v, k_v, v_v, enc_blocks, cache_slot,
+    hid_v, wq_v, wo_v, k_v, v_v, idx_s,
     norm_own, norm_got, q_own, q_out, q_oth, ctx_v, fin_out, fin_all,
     in_sem, ld_sem, send_sem, recv_sem,
 ):
@@ -51,12 +51,12 @@
     ld_v = pltpu.make_async_copy(vals, v_v, ld_sem.at[3])
     ld_wo = [
         pltpu.make_async_copy(
-            wo.at[:, pl.ds(dz * feats, feats)], wo_v.at[dz], ld_sem.at[4 + dz]
+            wo.at[:, pl.ds(dz * feats, feats)], wo_v.at[dz], ld_sem.at[4]
         )
         for dz in range(4)
     ]
-    ld_enc = pltpu.make_async_copy(enc_hbm, enc_blocks, ld_sem.at[8])
-    ld_slot = pltpu.make_async_copy(slot_hbm, cache_slot, ld_sem.at[9])
+    ld_enc = pltpu.make_async_copy(enc_hbm, idx_s.at[0], ld_sem.at[5])
+    ld_slot = pltpu.make_async_copy(slot_hbm, idx_s.at[1], ld_sem.at[5])
     for cp in [ld_hid, ld_enc, ld_slot, ld_wq]:
         cp.start()
 
@@ -74,8 +74,8 @@
     norm_own[0] = normed[:, :half]
     norm_own[1] = normed[:, half:]
 
-    ld_enc.wait()
-    ld_slot.wait()
+    wait_bytes(idx_s, ld_sem.at[5])
+    enc_blocks, cache_slot = idx_s.at[0], idx_s.at[1]
     slot_req = []
     for i in range(ROWS):
         mine = (w * DEPTH + d) * ROWS + i
@@ -139,7 +139,8 @@
     ctx_b = ctx_v[...].astype(jnp.bfloat16)
     here = z * WIDE + w
     for to_z in range(NARROW):
-        ld_wo[to_z].wait()
+        if to_z == 0:
+            wait_bytes(wo_v, ld_sem.at[4])
         block = jnp.dot(ctx_b, wo_v[to_z], preferred_element_type=jnp.float32).astype(jnp.bfloat16)
         fin_out[to_z] = block
         if to_z == 0:
@@ -152,6 +153,9 @@
             send(fin_out.at[to_z], fin_all.at[here], 3, peer(w, to_z, d))
 
     fin_all[here] = fin_out[z]
+    sent_a()
+    sent_q()
+    sent_o()
     wait_bytes(fin_all.at[pl.ds(0, NARROW * WIDE - 1)], recv_sem.at[3])
     rows = []
     for i in range(ROWS):
@@ -163,9 +167,6 @@
         rows.append(jnp.sum(jnp.where(row_id == slot % ROWS, pair, 0.0), axis=0, keepdims=True))
     out[...] = jnp.concatenate(rows, axis=0).astype(jnp.bfloat16)
 
-    sent_a()
-    sent_q()
-    sent_o()
     wait_bytes(fin_all.at[pl.ds(0, NARROW * WIDE - 1)], send_sem.at[3])
 
 
@@ -189,8 +190,7 @@
             pltpu.VMEM((NARROW, feats, feats), bf16),
             pltpu.VMEM(cache_keys.shape, bf16),
             pltpu.VMEM(cache_values.shape, bf16),
-            pltpu.SMEM(enc_blocks.shape, jnp.int32),
-            pltpu.SMEM(cache_slot.shape, jnp.int32),
+            pltpu.SMEM((2, *enc_blocks.shape), jnp.int32),
             pltpu.VMEM((2, rows, half), bf16),
             pltpu.VMEM((rows, half), bf16),
             pltpu.VMEM((WIDE, rows, feats), f32),
@@ -200,7 +200,7 @@
             pltpu.VMEM((NARROW, rows, feats), bf16),
             pltpu.VMEM((NARROW * WIDE, rows, feats), bf16),
             pltpu.SemaphoreType.REGULAR,
-            dma((10,)), dma((4,)), dma((4,)),
+            dma((6,)), dma((4,)), dma((4,)),
         ],
         compiler_params=pltpu.CompilerParams(
             collective_id=0, has_side_effects=True, vmem_limit_bytes=48 * 1024 * 1024

time: 24.9 us -> 24.8 us (level)
  no operation moved by 1% of the time
where the time goes in v7:
time: 24.8 us; the launch traced here: 24.7 us
  Pallas kernels  24.1 us (97%)
  local copies, waits for them, and re-layouts  0.6 us (2%)
    pallas_call x1, Pallas kernels, shards(): pl.pallas_call(kernel, out_shape=jax.ShapeDtypeStruct((rows, feats), bf16...  24.1 us
    unnamed x1, local copies, waits for them, and re-layouts  0.6 us

profile of v7, /device:TPU:1, one launch (start us, length us, event | category | flops | bytes accessed | tf_op | source)
XLA Modules:
  0.0 24.7 jit_solution(12086138348385122650)
XLA Ops:
  0.0 24.1 %shard_map.73 = bf16[2,1024]{1,0:T(2,128)(2,1)S(1)} custom-call(bf16[2,4096]{1,0:T(2,128)(2,1)} %hid.1, bf16[2048,1024]{1,0:T(8,128)(2,1)} %wq.1, bf16[1024,4096]{1,0:T(8,128)(2,1)} %wo.1, bf16[2,512,1024]{2,1,0:T(8,128)(2,1)} %keys.1, bf16[2,512,1024]{2,1,0:T(8,128)(2,1)} %vals.1, s32[64]{0:T(128)} %enc_hbm.1, s32[64]{0:T(128)} %slot_hbm.1), custom_call_target="tpu_custom_call" | custom-call | tf_op jit(solution)/shard_map/pallas_call | solution.py:182
  24.1 0.6 %copy.9 = bf16[2,1024]{1,0:T(2,128)(2,1)} copy(bf16[2,1024]{1,0:T(2,128)(2,1)S(1)} %shard_map.73) | data formatting | bytes 8192

commit v8 on v7

--- a/solution.py
+++ b/solution.py
@@ -122,8 +122,8 @@
     for i in range(ROWS):
         req = slot_req[i]
         src = req // (DEPTH * ROWS)
-        pair = (q_own[src] + q_oth[src]).astype(jnp.bfloat16).astype(jnp.float32)
-        query = jnp.sum(jnp.where(row_id == req % ROWS, pair, 0.0), axis=0, keepdims=True)
+        row = pl.ds(req % ROWS, 1)
+        query = (q_own[src, row] + q_oth[src, row]).astype(jnp.bfloat16).astype(jnp.float32)
         spread = jnp.where(own_head, query, 0.0).astype(jnp.bfloat16)
         score = lax.dot_general(
             spread, k_v[i], (((1,), (1,)), ((), ())), preferred_element_type=jnp.float32

time: 24.8 us -> 24.8 us (level)
  no operation moved by 1% of the time
where the time goes in v8:
time: 24.8 us; the launch traced here: 24.7 us
  Pallas kernels  24.1 us (97%)
  local copies, waits for them, and re-layouts  0.6 us (2%)
    pallas_call x1, Pallas kernels, shards(): pl.pallas_call(kernel, out_shape=jax.ShapeDtypeStruct((rows, feats), bf16...  24.1 us
    unnamed x1, local copies, waits for them, and re-layouts  0.6 us

profile of v8, /device:TPU:1, one launch (start us, length us, event | category | flops | bytes accessed | tf_op | source)
XLA Modules:
  0.0 24.7 jit_solution(18189130287793155949)
XLA Ops:
  0.0 24.1 %shard_map.73 = bf16[2,1024]{1,0:T(2,128)(2,1)S(1)} custom-call(bf16[2,4096]{1,0:T(2,128)(2,1)} %hid.1, bf16[2048,1024]{1,0:T(8,128)(2,1)} %wq.1, bf16[1024,4096]{1,0:T(8,128)(2,1)} %wo.1, bf16[2,512,1024]{2,1,0:T(8,128)(2,1)} %keys.1, bf16[2,512,1024]{2,1,0:T(8,128)(2,1)} %vals.1, s32[64]{0:T(128)} %enc_hbm.1, s32[64]{0:T(128)} %slot_hbm.1), custom_call_target="tpu_custom_call" | custom-call | tf_op jit(solution)/shard_map/pallas_call | solution.py:182
  24.1 0.6 %copy.9 = bf16[2,1024]{1,0:T(2,128)(2,1)} copy(bf16[2,1024]{1,0:T(2,128)(2,1)S(1)} %shard_map.73) | data formatting | bytes 8192
